TPU v7x, 256 devices: a whole 4x4x8 slice. The times are simulated.
256 devices in a mesh: list: 32 (over x, y, core), rep: 8 (over z).
Axes of the slice: x: 4, y: 4, z: 8, core: 2. Of those that a mesh axis runs over, the one named last changes fastest.
Arguments:
- memory_rows: bfloat16 [65536, 1024], P(('list', 'rep'))
- list_owner: int32 [65536, 1], P(('list', 'rep')), may hold values from 0 to 31; in each aligned block of 256 rows (0 to 255, 256 to 511, ...) at most 32 rows name the same one
- list_slot: int32 [65536], P(('list', 'rep')), may hold values from 0 to 2047
- pq_codes: int32 [65536, 16], P(('list', 'rep')), may hold values from 0 to 255
- valid_rows: int32 [256], P(('list', 'rep')), may hold values from 128 to 256
- centroids: bfloat16 [65536, 1024], P('list'), may hold values from -3 to 3
- codebook: float32 [16, 256, 64], replicated
Outputs:
- new_codebook: float32 [16, 256, 64], P('rep')
- row_error: float32 [65536], P(('list', 'rep'))
Inputs may be any that keep to these rules, and one draw needn't show every extreme that they name: `list_owner`: the rows of one device name one index of list at most 32 times, and some device's rows name one exactly 32 times.
All inputs are finite; a program needn't handle non-finite values.
Results may differ from a plain program's by a relative error of at most 0.0038.
Values may be sent and summed in bfloat16 or wider, within the bound.
A program may use at most 128 MiB of HBM per device.

v0:
```python
import jax
import jax.numpy as jnp
from jax import lax
from jax.sharding import PartitionSpec as P

prior_weight = 4.0


def code_statistics(residual, pq_codes, is_live, codebook):
    row_count = residual.shape[0]
    subspaces = codebook.shape[0]
    code_count = codebook.shape[1]
    width_sub = codebook.shape[2]
    residual = jnp.where(is_live[:, None], residual, 0.0)
    recon = codebook[jnp.arange(subspaces)[None, :], pq_codes].reshape(
        row_count, subspaces * width_sub
    )
    row_error = jnp.where(is_live, jnp.mean((residual - recon) ** 2, axis=1), 0.0)
    rounded = (
        residual.astype(jnp.bfloat16).reshape(row_count, subspaces, width_sub).transpose(1, 0, 2)
    )
    codes_major = pq_codes.T

    def per_subspace(item):
        code_col, part_rows = item
        onehot = ((code_col[:, None] == jnp.arange(code_count)[None, :]) & is_live[:, None]).astype(
            jnp.bfloat16
        )
        sums_one = lax.dot_general(
            onehot, part_rows, (((0,), (0,)), ((), ())), preferred_element_type=jnp.float32
        )
        counts_one = jnp.sum(onehot.astype(jnp.float32), axis=0)
        return (sums_one, counts_one)

    sums, counts = lax.map(per_subspace, (codes_major, rounded))
    return (row_error, sums, counts)


def body(memory_rows, list_owner, list_slot, pq_codes, valid_rows, centroids, codebook):
    row_count = memory_rows.shape[0]
    width = memory_rows.shape[1]
    list_count = centroids.shape[0]
    owners = lax.axis_size("list")
    capacity = 4 * row_count // owners
    is_valid = jnp.arange(row_count) < valid_rows[0]
    target = list_owner[:, 0]
    onehot_dest = ((target[:, None] == jnp.arange(owners)[None, :]) & is_valid[:, None]).astype(
        jnp.int32
    )
    before = jnp.cumsum(onehot_dest, axis=0) - onehot_dest
    slot_rank = jnp.sum(before * onehot_dest, axis=1)
    position = jnp.where(is_valid, target * capacity + slot_rank, owners * capacity)
    taken = jnp.clip(position, 0, owners * capacity - 1)
    total_slots = owners * capacity
    send_rows = (
        jnp.zeros((total_slots, width), jnp.bfloat16).at[position].set(memory_rows, mode="drop")
    )
    send_slot = jnp.full((total_slots,), -1, jnp.int32).at[position].set(list_slot, mode="drop")
    send_codes = (
        jnp.zeros((total_slots, pq_codes.shape[1]), jnp.int32)
        .at[position]
        .set(pq_codes, mode="drop")
    )
    got_rows, got_slot, got_codes = (
        lax.all_to_all(
            send_rows.reshape(owners, capacity, width),
            "list",
            split_axis=0,
            concat_axis=0,
            tiled=True,
        ),
        lax.all_to_all(
            send_slot.reshape(owners, capacity), "list", split_axis=0, concat_axis=0, tiled=True
        ),
        lax.all_to_all(
            send_codes.reshape(owners, capacity, pq_codes.shape[1]),
            "list",
            split_axis=0,
            concat_axis=0,
            tiled=True,
        ),
    )
    got_rows = got_rows.reshape(total_slots, width)
    got_slot = got_slot.reshape(total_slots)
    got_codes = got_codes.reshape(total_slots, pq_codes.shape[1])
    is_live = got_slot >= 0
    centre = centroids[jnp.clip(got_slot, 0, list_count - 1)].astype(jnp.float32)
    residual = got_rows.astype(jnp.float32) - centre
    slot_error, sums, counts = code_statistics(residual, got_codes, is_live, codebook)
    returned = lax.all_to_all(
        slot_error.reshape(owners, capacity), "list", split_axis=0, concat_axis=0, tiled=True
    )
    row_error = jnp.where(is_valid, returned.reshape(total_slots)[taken], 0.0)
    subspaces = codebook.shape[0]
    replicas = lax.axis_size("rep")
    share = subspaces // replicas
    first_sub = lax.axis_index("rep") * share
    sums_all, counts_all = lax.psum((sums, counts), ("list", "rep"))
    sums_mine = lax.dynamic_slice_in_dim(sums_all, first_sub, share, 0)
    counts_mine = lax.dynamic_slice_in_dim(counts_all, first_sub, share, 0)
    old_mine = lax.dynamic_slice_in_dim(codebook, first_sub, share, 0)
    new_codebook = (sums_mine + prior_weight * old_mine) / (counts_mine[:, :, None] + prior_weight)
    return (new_codebook, row_error)


def solution(mesh):
    in_specs = (
        P(("list", "rep"), None),
        P(("list", "rep"), None),
        P(("list", "rep")),
        P(("list", "rep"), None),
        P(("list", "rep")),
        P("list", None),
        P(),
    )
    out_specs = (P("rep", None, None), P(("list", "rep")))
    return jax.shard_map(body, mesh=mesh, in_specs=in_specs, out_specs=out_specs, check_vma=False)
```

profile of v0, /device:TPU:2, one launch (start us, length us, event | category | flops | bytes accessed | tf_op | source)
XLA Modules:
  0.0 582.1 jit_solution(2420515403371690203)
XLA Ops:
  13.1 7.6 %all-to-all-start.1 = ((s32[32,1,32]{2,1,0:T(1,128)}), s32[32,1,32]{2,1,0:T(1,128)S(1)}, u32[]{:S(2)}, u32[]{:S(2)}) async-start(s32[32,1,32]{2,1,0:T(1,128)} %all_to_all.17), calls=%async_computation.1 | async-start | bytes 32768 | tf_op jit(solution)/shard_map/all_to_all | solution.py:72
  23.9 3.1 all-to-all-done.1
  26.9 5.0 all-to-all-start
  31.9 3.7 scatter_custom_fusion.2
  35.6 2.7 all-to-all-done
  38.3 5.8 %all-to-all-start.2 = ((bf16[32,32,1024]{2,1,0:T(8,128)(2,1)}), bf16[32,32,1024]{2,1,0:T(8,128)(2,1)}, u32[]{:S(2)}, u32[]{:S(2)}) async-start(bf16[32,32,1024]{2,1,0:T(8,128)(2,1)} %bitcast.13), calls=%async_computation.2 | async-start | bytes 4194304 | tf_op jit(solution)/shard_map/all_to_all | solution.py:65
  45.2 8.8 %gather_fusion = bf16[1024,1024]{1,0:T(8,128)(2,1)} fusion(bf16[2048,1024]{1,0:T(8,128)(2,1)} %param.14, s32[1024]{0:T(1024)S(1)} %broadcast_clamp_fusion.1), kind=kCustom, calls=%fused_computation | custom fusion | bytes 4198400 | tf_op jit(solution)/shard_map/gather | solution.py:87
  53.9 4.1 copy.44
  58.0 4.0 convert_element_type.53
  62.0 8.1 %copy.45 = f32[1024,16,64]{2,1,0:T(8,128)} copy(f32[1024,16,64]{0,2,1:T(8,128)} %bitcast.73) | data formatting | bytes 8388608 | tf_op jit(solution)/shard_map/convert_element_type | solution.py:87
  72.4 176.0 %gather_fusion.1 = f32[16384,64]{1,0:T(8,128)} fusion(f32[16,256,64]{2,1,0:T(8,128)S(1)} %copy.49, s32[16384]{0:T(1024)S(1)} %reshape.188), kind=kCustom, calls=%fused_computation.1 | custom fusion | bytes 8519680 | tf_op jit(solution)/shard_map/gather | solution.py:15
  248.5 7.6 %gather.13 = f32[32,32,1024]{2,1,0:T(8,128)} reshape(f32[16384,64]{1,0:T(8,128)} %gather_fusion.1) | data formatting | bytes 8388608 | tf_op jit(solution)/shard_map/gather | solution.py:15
  256.1 6.9 %reshape.177 = f32[1024,16,64]{2,1,0:T(8,128)} reshape(bf16[32,32,1024]{2,1,0:T(8,128)(2,1)} %all-to-all-done.2) | data formatting | bytes 6291456 | tf_op jit(solution)/shard_map/convert_element_type | solution.py:88
  262.9 7.7 %fusion.9 = bf16[16,1024,64]{2,0,1:T(8,128)(2,1)S(1)} fusion(f32[1024,16,64]{2,1,0:T(8,128)} %reshape.177, f32[1024,16,64]{2,1,0:T(8,128)} %copy.45, pred[1024]{0:T(1024)(128)(4,1)S(1)} %ge.17), kind=kLoop, calls=%fused_computation.19 | loop fusion | flops 3145728 | bytes 10486784 | tf_op jit(solution)/shard_map/transpose | solution.py:20
  270.6 3.0 copy.46
  273.6 40.9 %while.12 = (s32[]{:T(128)}, f32[16,256,64]{1,2,0:T(8,128)}, f32[16,256]{1,0:T(8,128)S(1)}, s32[16,1024]{1,0:T(8,128)S(1)}, pred[1024]{0:T(1024)(128)(4,1)S(1)},...) while((s32[]{:T(128)}, f32[16,256,64]{1,2,0:T(8,128)}, f32[16,256]{1,0:T(8,128)S(1)}, ...), condition=%wide.region_8.9_spmd, body=%wide.region_6.8_spmd.sunk | while | flops 35389184 | bytes 350301 | solution.py:35
  276.2 2.1 fusion.31
  278.8 2.1 fusion.31
  283.9 2.1 fusion.31
  289.0 2.1 fusion.31
  291.5 2.1 fusion.31
  294.1 2.1 fusion.31
  296.6 2.1 fusion.31
  299.2 2.1 fusion.31
  301.8 2.1 fusion.31
  304.3 2.1 fusion.31
  306.9 2.1 fusion.31
  312.0 2.1 fusion.31
  314.6 5.1 multiply_reduce_fusion
  320.3 7.4 %all-to-all-start.3 = ((f32[32,1,32]{2,1,0:T(1,128)}), f32[32,1,32]{2,1,0:T(1,128)S(1)}, u32[]{:S(2)}, u32[]{:S(2)}) async-start(f32[32,1,32]{2,1,0:T(1,128)} %bitcast.21), calls=%async_computation.3 | async-start | bytes 32768 | tf_op jit(solution)/shard_map/all_to_all | solution.py:90
  327.7 79.8 %psum.15 = f32[16,256]{1,0:T(8,128)S(1)} all-reduce(f32[16,256]{1,0:T(8,128)S(1)} %get-tuple-element.36), channel_id=1, replica_groups=mesh['list'=32,'rep'=8] {'list','rep'}, use_global_device_ids=true, to_apply=%region_10.11 | all-reduce | flops 4096 | bytes 32768 | tf_op jit(solution)/shard_map/psum | solution.py:98
  410.7 162.9 %all-reduce.2.cloned.1.call-done = f32[16,256,64]{1,2,0:T(8,128)} async-done(((f32[16,256,64]{1,2,0:T(8,128)}), f32[16,256,64]{1,2,0:T(8,128)}) %all-reduce.2.cloned.1.call-update) | async-done | bytes 1048592 | tf_op jit(solution)/shard_map/psum | solution.py:98
  (102 shorter events, 32.0 us)
Async XLA Ops:
  9.1 35.3 %copy-start = (f32[16,256,64]{1,2,0:T(8,128)S(1)}, f32[16,256,64]{1,2,0:T(8,128)}, u32[]{:S(2)}) copy-start(f32[16,256,64]{1,2,0:T(8,128)} %param.15) | copy-start | bytes 3145732
  13.1 13.8 %all-to-all-start.1 = ((s32[32,1,32]{2,1,0:T(1,128)}), s32[32,1,32]{2,1,0:T(1,128)S(1)}, u32[]{:S(2)}, u32[]{:S(2)}) async-start(s32[32,1,32]{2,1,0:T(1,128)} %all_to_all.17), calls=%async_computation.1 | async-start | bytes 32768 | tf_op jit(solution)/shard_map/all_to_all | solution.py:72
  26.9 11.4 %all-to-all-start = ((s32[32,1,512]{2,1,0:T(1,128)}), s32[32,1,512]{2,1,0:T(1,128)S(1)}, u32[]{:S(2)}, u32[]{:S(2)}) async-start(s32[32,1,512]{2,1,0:T(1,128)} %reshape.243), calls=%async_computation | async-start | bytes 131072 | tf_op jit(solution)/shard_map/all_to_all | solution.py:75
  38.3 217.7 %all-to-all-start.2 = ((bf16[32,32,1024]{2,1,0:T(8,128)(2,1)}), bf16[32,32,1024]{2,1,0:T(8,128)(2,1)}, u32[]{:S(2)}, u32[]{:S(2)}) async-start(bf16[32,32,1024]{2,1,0:T(8,128)(2,1)} %bitcast.13), calls=%async_computation.2 | async-start | bytes 4194304 | tf_op jit(solution)/shard_map/all_to_all | solution.py:65
  44.2 529.5 %all-reduce.2.cloned.1.call-start = ((), (), s32[]{:S(2)}) async-start(), calls=%async_computation.4 | async-start | bytes 2097152 | tf_op jit(solution)/shard_map/psum | solution.py:98
  320.3 87.2 %all-to-all-start.3 = ((f32[32,1,32]{2,1,0:T(1,128)}), f32[32,1,32]{2,1,0:T(1,128)S(1)}, u32[]{:S(2)}, u32[]{:S(2)}) async-start(f32[32,1,32]{2,1,0:T(1,128)} %bitcast.21), calls=%async_computation.3 | async-start | bytes 32768 | tf_op jit(solution)/shard_map/all_to_all | solution.py:90
Sparse Core Ops, SparseCore 0:
  314.7 258.9 all-reduce.1
where the time goes:
time: 584 us; the launch traced here: 582 us
  local copies, waits for them, and re-layouts  229 us (39%)
  waiting for transfers between devices  169 us (29%)
  blocking collectives  79.8 us (14%)
  matrix products  34 us (6%)
  other arithmetic  29.6 us (5%)
  starting transfers between devices  26.1 us (4%)
  between operations  14.9 us (3%)
    gather x2, local copies, waits for them, and re-layouts, code_statistics(): codebook[jnp.arange(subspaces)[None, :], pq_codes]  184 us
    psum x1, waiting for transfers between devices, body(): sums_all, counts_all = lax.psum((sums, counts), ('list', 'rep'))  163 us
    psum x1, blocking collectives, body(): sums_all, counts_all = lax.psum((sums, counts), ('list', 'rep'))  79.8 us
    dot_general x16, matrix products, per_subspace(): lax.dot_general(onehot, part_rows, (((0,), (0,)), ((), ())), preferred_el...  34 us
    convert_element_type x2, local copies, waits for them, and re-layouts, body(): centroids[jnp.clip(got_slot, 0, list_count - 1)].astype(jnp.float32)  12.2 us
  transfers between devices with their start and end apart: 5, of which 3 were waited for; matrix products, arithmetic and copies ran while one was open for 39% of the time, Pallas kernels for 0%

commit v1 on v0

--- a/solution.py
+++ b/solution.py
@@ -1,9 +1,17 @@
+import functools
 import jax
 import jax.numpy as jnp
 from jax import lax
 from jax.sharding import PartitionSpec as P
 
 prior_weight = 4.0
+
+
+def digits_shape(raw, axis_name, axis_tag):
+    return jax.lax.psum(jax.lax.psum(raw, axis_tag), axis_name)
+
+
+follow_words = functools.partial(digits_shape, axis_name="list", axis_tag="rep")
 
 
 def code_statistics(residual, pq_codes, is_live, codebook):
@@ -95,7 +103,7 @@
     replicas = lax.axis_size("rep")
     share = subspaces // replicas
     first_sub = lax.axis_index("rep") * share
-    sums_all, counts_all = lax.psum((sums, counts), ("list", "rep"))
+    sums_all, counts_all = follow_words((sums, counts))
     sums_mine = lax.dynamic_slice_in_dim(sums_all, first_sub, share, 0)
     counts_mine = lax.dynamic_slice_in_dim(counts_all, first_sub, share, 0)
     old_mine = lax.dynamic_slice_in_dim(codebook, first_sub, share, 0)

time: 584 us -> 498 us (0.85)
  the two profiles are of different devices: /device:TPU:2 before, /device:TPU:0 now
where the time goes in v1:
time: 498 us; the launch traced here: 497 us
  local copies, waits for them, and re-layouts  227 us (46%)
  blocking collectives  157 us (32%)
  matrix products  34.1 us (7%)
  other arithmetic  29.6 us (6%)
  starting transfers between devices  18.3 us (4%)
  waiting for transfers between devices  15.8 us (3%)
  between operations  14.9 us (3%)
    gather x2, local copies, waits for them, and re-layouts, code_statistics(): codebook[jnp.arange(subspaces)[None, :], pq_codes]  184 us
    psum x2, blocking collectives, digits_shape(): return jax.lax.psum(jax.lax.psum(raw, axis_tag), axis_name)  157 us
    dot_general x16, matrix products, per_subspace(): lax.dot_general(onehot, part_rows, (((0,), (0,)), ((), ())), preferred_el...  34.1 us
    convert_element_type x2, local copies, waits for them, and re-layouts, body(): centroids[jnp.clip(got_slot, 0, list_count - 1)].astype(jnp.float32)  11.3 us
  transfers between devices with their start and end apart: 6, of which 3 were waited for; matrix products, arithmetic and copies ran while one was open for 45% of the time, Pallas kernels for 0%

profile of v1, /device:TPU:0, one launch (start us, length us, event | category | flops | bytes accessed | tf_op | source)
XLA Modules:
  0.0 496.7 jit_solution(12410762649620290862)
XLA Ops:
  13.1 5.6 %all-to-all-start.1 = ((s32[32,1,32]{2,1,0:T(1,128)}), s32[32,1,32]{2,1,0:T(1,128)S(1)}, u32[]{:S(2)}, u32[]{:S(2)}) async-start(s32[32,1,32]{2,1,0:T(1,128)} %all_to_all.17), calls=%async_computation.1 | async-start | bytes 32768 | tf_op jit(solution)/shard_map/all_to_all | solution.py:80
  21.7 4.3 all-to-all-done.1
  26.0 3.9 all-to-all-start
  29.9 3.8 scatter_custom_fusion.2
  33.7 3.7 all-to-all-done
  37.4 4.8 all-to-all-start.2
  42.5 7.7 %gather_fusion = bf16[1024,1024]{1,0:T(8,128)(2,1)S(1)} fusion(bf16[2048,1024]{1,0:T(8,128)(2,1)} %param.14, s32[1024]{0:T(1024)S(1)} %broadcast_clamp_fusion.1), kind=kCustom, calls=%fused_computation | custom fusion | bytes 4198400 | tf_op jit(solution)/shard_map/gather | solution.py:95
  50.3 3.2 copy.44
  53.4 8.1 %copy.45 = f32[1024,16,64]{2,1,0:T(8,128)} copy(f32[1024,16,64]{0,2,1:T(8,128)} %bitcast.73) | data formatting | bytes 8388608 | tf_op jit(solution)/shard_map/convert_element_type | solution.py:95
  63.3 7.7 %all-to-all-done.2 = bf16[32,32,1024]{2,1,0:T(8,128)(2,1)} async-done(((bf16[32,32,1024]{2,1,0:T(8,128)(2,1)}), bf16[32,32,1024]{2,1,0:T(8,128)(2,1)}, u32[]{:S(2)}, u32[]{:S(2)}) %all-to-all-start.2) | async-done | bytes 2097184 | tf_op jit(solution)/shard_map/all_to_all | solution.py:73
  71.0 6.9 %reshape.177 = f32[1024,16,64]{2,1,0:T(8,128)} reshape(bf16[32,32,1024]{2,1,0:T(8,128)(2,1)} %all-to-all-done.2) | data formatting | bytes 6291456 | tf_op jit(solution)/shard_map/convert_element_type | solution.py:96
  77.9 7.7 %fusion.9 = bf16[16,1024,64]{2,0,1:T(8,128)(2,1)S(1)} fusion(f32[1024,16,64]{2,1,0:T(8,128)} %reshape.177, f32[1024,16,64]{2,1,0:T(8,128)} %copy.45, pred[1024]{0:T(1024)(128)(4,1)S(1)} %ge.17), kind=kLoop, calls=%fused_computation.19 | loop fusion | flops 3145728 | bytes 10486784 | tf_op jit(solution)/shard_map/transpose | solution.py:28
  85.6 3.0 copy.46
  88.6 41.0 %while.12 = (s32[]{:T(128)}, f32[16,256,64]{1,2,0:T(8,128)}, f32[16,256]{1,0:T(8,128)S(1)}, s32[16,1024]{1,0:T(8,128)S(1)}, pred[1024]{0:T(1024)(128)(4,1)S(1)},...) while((s32[]{:T(128)}, f32[16,256,64]{1,2,0:T(8,128)}, f32[16,256]{1,0:T(8,128)S(1)}, ...), condition=%wide.region_8.9_spmd, body=%wide.region_6.8_spmd.sunk | while | flops 35389184 | bytes 350301 | solution.py:43
  88.6 2.2 fusion.31
  93.8 2.1 fusion.31
  96.4 2.1 fusion.31
  98.9 2.1 fusion.31
  101.5 2.1 fusion.31
  106.6 2.1 fusion.31
  111.7 2.1 fusion.31
  116.8 2.1 fusion.31
  119.4 2.1 fusion.31
  121.9 2.1 fusion.31
  124.5 2.1 fusion.31
  130.3 4.0 convert_element_type.53
  134.9 176.0 %gather_fusion.1 = f32[16384,64]{1,0:T(8,128)} fusion(f32[16,256,64]{2,1,0:T(8,128)S(1)} %copy.49, s32[16384]{0:T(1024)S(1)} %reshape.188), kind=kCustom, calls=%fused_computation.1 | custom fusion | bytes 8519680 | tf_op jit(solution)/shard_map/gather | solution.py:23
  310.9 7.6 %gather.13 = f32[32,32,1024]{2,1,0:T(8,128)} reshape(f32[16384,64]{1,0:T(8,128)} %gather_fusion.1) | data formatting | bytes 8388608 | tf_op jit(solution)/shard_map/gather | solution.py:23
  318.6 5.1 %multiply_reduce_fusion = f32[32,32]{1,0:T(8,128)S(1)} fusion(f32[32,32,1024]{2,1,0:T(8,128)} %gather.13, f32[32,32,1024]{2,1,0:T(8,128)} %bitcast.74, pred[32,32]{1,0:T(8,128)(4,1)S(1)} %fusion.25, bf16[32,32,1024]{2,1,0:T(8,128)(2,1)} %all-to-all-done.2), kind=kLoop, calls=%fused_computation.20 | loop fusion | flops 6290432 | bytes 10490880 | tf_op jit(solution)/shard_map/reduce_sum | solution.py:26
  324.3 3.8 all-to-all-start.3
  328.1 32.8 %psum.30 = f32[16,256]{1,0:T(8,128)S(1)} all-reduce(f32[16,256]{1,0:T(8,128)S(1)} %get-tuple-element.36), channel_id=1, replica_groups=mesh['list'=32,'rep'=8] {'rep'}, use_global_device_ids=true, to_apply=%region_11.12 | all-reduce | flops 4096 | bytes 32768 | tf_op jit(solution)/shard_map/psum | solution.py:11
  360.9 124.1 %psum.31 = f32[16,256]{1,0:T(8,128)S(1)} all-reduce(f32[16,256]{1,0:T(8,128)S(1)} %psum.30), channel_id=1, replica_groups=mesh['list'=32,'rep'=8] {'list'}, use_global_device_ids=true, to_apply=%region_12.13 | all-reduce | flops 4096 | bytes 32768 | tf_op jit(solution)/shard_map/psum | solution.py:11
  (108 shorter events, 34.1 us)
Async XLA Ops:
  13.1 13.0 %all-to-all-start.1 = ((s32[32,1,32]{2,1,0:T(1,128)}), s32[32,1,32]{2,1,0:T(1,128)S(1)}, u32[]{:S(2)}, u32[]{:S(2)}) async-start(s32[32,1,32]{2,1,0:T(1,128)} %all_to_all.17), calls=%async_computation.1 | async-start | bytes 32768 | tf_op jit(solution)/shard_map/all_to_all | solution.py:80
  26.0 11.4 %all-to-all-start = ((s32[32,1,512]{2,1,0:T(1,128)}), s32[32,1,512]{2,1,0:T(1,128)S(1)}, u32[]{:S(2)}, u32[]{:S(2)}) async-start(s32[32,1,512]{2,1,0:T(1,128)} %reshape.243), calls=%async_computation | async-start | bytes 131072 | tf_op jit(solution)/shard_map/all_to_all | solution.py:83
  37.4 33.6 %all-to-all-start.2 = ((bf16[32,32,1024]{2,1,0:T(8,128)(2,1)}), bf16[32,32,1024]{2,1,0:T(8,128)(2,1)}, u32[]{:S(2)}, u32[]{:S(2)}) async-start(bf16[32,32,1024]{2,1,0:T(8,128)(2,1)} %bitcast.13), calls=%async_computation.2 | async-start | bytes 4194304 | tf_op jit(solution)/shard_map/all_to_all | solution.py:73
  42.2 281.5 %all-reduce.3.cloned.1.call-start = ((), (), s32[]{:S(2)}) async-start(), calls=%async_computation.4 | async-start | bytes 2097152 | tf_op jit(solution)/shard_map/psum | solution.py:11
  50.2 11.3 %copy-start = (bf16[1024,1024]{1,0:T(8,128)(2,1)}, bf16[1024,1024]{1,0:T(8,128)(2,1)S(1)}, u32[]{:S(2)}) copy-start(bf16[1024,1024]{1,0:T(8,128)(2,1)S(1)} %gather_fusion) | copy-start | bytes 6291460
  88.6 41.1 %copy-start.1 = (f32[16,256,64]{1,2,0:T(8,128)S(1)}, f32[16,256,64]{1,2,0:T(8,128)}, u32[]{:S(2)}) copy-start(f32[16,256,64]{1,2,0:T(8,128)} %param.15) | copy-start | bytes 3145732
  129.6 358.6 %all-reduce.5.cloned.1.call-start = ((), (), s32[]{:S(2)}) async-start(), calls=%async_computation.5 | async-start | bytes 2097152 | tf_op jit(solution)/shard_map/psum | solution.py:11
  324.3 160.7 %all-to-all-start.3 = ((f32[32,1,32]{2,1,0:T(1,128)}), f32[32,1,32]{2,1,0:T(1,128)S(1)}, u32[]{:S(2)}, u32[]{:S(2)}) async-start(f32[32,1,32]{2,1,0:T(1,128)} %bitcast.21), calls=%async_computation.3 | async-start | bytes 32768 | tf_op jit(solution)/shard_map/all_to_all | solution.py:98
Sparse Core Ops, SparseCore 0:
  129.7 75.0 all-reduce.2
  323.8 114.1 all-reduce.4
